TPU v7x, 32 devices: a whole 2x2x4 slice. The times are simulated.
32 devices in a mesh: vol: 8 (over z, x), nar: 4 (over y, core).
Axes of the slice: x: 2, y: 2, z: 4, core: 2. Of those that a mesh axis runs over, the one named last changes fastest.
Arguments:
- series: bfloat16 [2048, 2048], P(('vol', 'nar')), may hold values from -6 to 6
- send_rows: int32 [8, 4, 16], P('vol', 'nar'), may hold values from -1 to 63, as said below
- bin_counts: int32 [4], replicated, may hold values from 1 to 128, 256 in all
- observer_cells: int32 [2, 512], replicated, may hold values from 0 to 127
Outputs:
- spectra_out: float32 [4, 128, 2, 512], P('nar', 'vol')
Inputs may be any that keep to these rules, and one draw needn't show every extreme that they name: `send_rows`: entry (u, n, k) names the row of device (u, n)'s 64 rows of series for slot k mod 2 bound for the patch owner at vol index k // 2 and nar index n, or is -1 for an empty slot; one device never names a row twice. Nar index m owns bin_counts[m] bins in order, from the sum of the counts before m on; some owner holds exactly 128 bins. `observer_cells`: row 0 holds polar indices, row 1 azimuthal indices.
All inputs are finite; a program needn't handle non-finite values.
Results may differ from a plain program's by a relative error of at most 0.0043.
Values may be sent and summed in bfloat16 or wider, within the bound.
No kernel may reach another device: no remote copies, remote signals or barrier semaphores. Data moves between devices by JAX's collectives and lax.ppermute only.
A program may use at most 64 MiB of HBM per device.

v0:
```python
import math
import jax
import jax.numpy as jnp
from jax import lax
from jax.sharding import PartitionSpec as P

NF = 256
NQ = 4
WAVE_STEP = 0.05


def dft_table(bin_ids, keep_bin, time_len):
    time_steps = jnp.arange(time_len, dtype=jnp.int32)
    frequency = bin_ids + 1
    phase_turns = time_steps[:, None] * frequency[None, :] % time_len
    angle_grid = phase_turns.astype(jnp.float32) * (2.0 * math.pi / time_len)
    dft_grid = jnp.stack([jnp.cos(angle_grid), -jnp.sin(angle_grid)], axis=-1)
    dft_grid = jnp.where(keep_bin[None, :, None], dft_grid, jnp.float32(0.0))
    return dft_grid.reshape(time_len, 2 * bin_ids.shape[0]).astype(jnp.bfloat16)


def positions(point_list):
    beside_all = (point_list * 1597 % 8191).astype(jnp.float32) * (2.0 * math.pi / 8191.0)
    jitter = (point_list * 613 % 127).astype(jnp.float32) * (0.37 / 127.0)
    axial = (point_list // 128).astype(jnp.float32) * 0.5 + jitter
    return (20.0 * jnp.cos(beside_all), 20.0 * jnp.sin(beside_all), axial)


def directions(obs_cells):
    polar_angle = (obs_cells[0].astype(jnp.float32) + 0.5) * (math.pi / 128.0)
    azimuth = obs_cells[1].astype(jnp.float32) * (2.0 * math.pi / 128.0)
    return (
        jnp.sin(polar_angle) * jnp.cos(azimuth),
        jnp.sin(polar_angle) * jnp.sin(azimuth),
        jnp.cos(polar_angle),
    )


def project(facing, place_xyz):
    dotted = facing[0][:, None] * place_xyz[0][None, :] + facing[1][:, None] * place_xyz[1][None, :]
    return dotted + facing[2][:, None] * place_xyz[2][None, :]


def kernels(bin_ids, dotted):
    wavenumber = (bin_ids.astype(jnp.float32) + 1.0) * WAVE_STEP
    phase_grid = wavenumber[:, None, None] * dotted[None]
    return jnp.concatenate([jnp.cos(phase_grid), jnp.sin(phase_grid)], axis=1).astype(jnp.bfloat16)


def combine(products, bin_ids, facing, norm_scale):
    observers = facing[0].shape[0]
    bin_total = bin_ids.shape[0]
    cos_part = products[:, :observers].reshape(bin_total, observers, NQ, 2)
    sine_part = products[:, observers:].reshape(bin_total, observers, NQ, 2)
    real_part = cos_part[..., 0] + sine_part[..., 1]
    imag_part = cos_part[..., 1] - sine_part[..., 0]
    weights = jnp.stack([jnp.ones_like(facing[0]), facing[0], facing[1], facing[2]], axis=-1)
    real_sum = jnp.sum(real_part * weights[None], axis=-1)
    imag_sum = jnp.sum(imag_part * weights[None], axis=-1)
    amplitude = (bin_ids.astype(jnp.float32) + 1.0) * (norm_scale / NF)
    return jnp.stack([-amplitude[:, None] * imag_sum, amplitude[:, None] * real_sum], axis=1)


def apply_green(bin_ids, spec_block, dotted, facing, norm_scale):
    green_grid = kernels(bin_ids, dotted)
    products = jnp.einsum(
        "bxp,bcp->bxc", green_grid, spec_block, preferred_element_type=jnp.float32
    )
    return combine(products, bin_ids, facing, norm_scale)


def per_device(series, send_rows, bin_counts, observer_cells):
    vol_count = lax.axis_size("vol")
    nar_count = lax.axis_size("nar")
    vol_index = lax.axis_index("vol")
    nar_index = lax.axis_index("nar")
    bin_cap = vol_count * max(1, 2 * NF // (nar_count * vol_count))
    time_len = series.shape[1] // NQ
    slot_total = send_rows.shape[2]
    slot_width = slot_total // vol_count
    listing = send_rows.reshape(-1)
    picked = jnp.take(series, jnp.maximum(listing, 0), axis=0)
    packed = jnp.where((listing >= 0)[:, None], picked, jnp.zeros((), series.dtype))
    arrived = lax.all_to_all(packed, "vol", split_axis=0, concat_axis=0, tiled=True)
    starts = jnp.cumsum(bin_counts) - bin_counts
    own_start = starts[nar_index]
    own_count = bin_counts[nar_index]
    dft_scale = 1.0 / math.sqrt(time_len)
    within = jnp.arange(bin_cap, dtype=jnp.int32)
    own_table = dft_table(own_start + within, within < own_count, time_len)
    row_piece = lax.all_gather(arrived, "nar", axis=0, tiled=True)
    rows_here = row_piece.shape[0]
    spectral = jnp.dot(
        row_piece.reshape(rows_here * NQ, time_len), own_table, preferred_element_type=jnp.float32
    )
    spectral = (spectral * dft_scale).astype(jnp.bfloat16).reshape(rows_here, NQ, bin_cap, 2)
    spectra = spectral.transpose(2, 1, 3, 0).reshape(bin_cap, 2 * NQ, rows_here)
    local_points = nar_count * slot_total

    def point_ids(vol_owner, flat_index):
        nar_source = flat_index // slot_total
        remain = flat_index % slot_total
        vol_source = remain // slot_width
        within_slot = remain % slot_width
        return (
            (vol_source * nar_count + nar_source) * vol_count + vol_owner
        ) * slot_width + within_slot

    norm_scale = 1.0 / math.sqrt(vol_count * nar_count * slot_total)
    facing = directions(observer_cells)
    share_rows = bin_cap // vol_count
    regrouped = lax.all_to_all(spectra, "vol", split_axis=0, concat_axis=2, tiled=True)
    bin_ids = own_start + vol_index * share_rows + jnp.arange(share_rows, dtype=jnp.int32)
    span_points = local_points * max(1, vol_count // 8)
    turn_count = vol_count * local_points // span_points

    def add_block(turn_index, running):
        first_point = turn_index * span_points
        spec_block = lax.dynamic_slice_in_dim(regrouped, first_point, span_points, 2)
        flat_index = first_point + jnp.arange(span_points, dtype=jnp.int32)
        point_list = point_ids(flat_index // local_points, flat_index % local_points)
        dotted = project(facing, positions(point_list))
        return running + apply_green(bin_ids, spec_block, dotted, facing, norm_scale)

    result = lax.fori_loop(
        0, turn_count, add_block, jnp.zeros((share_rows, 2, observer_cells.shape[1]), jnp.float32)
    )
    return result.reshape(1, share_rows, 2, result.shape[-1])


def solution(mesh):
    placed = (P(("vol", "nar"), None), P("vol", "nar", None), P(), P())
    return jax.shard_map(
        per_device,
        mesh=mesh,
        in_specs=placed,
        out_specs=P("nar", "vol", None, None),
        check_vma=False,
    )
```

profile of v0, /device:TPU:0, one launch (start us, length us, event | category | flops | bytes accessed | tf_op | source)
XLA Modules:
  0.0 133.8 jit_solution(10418153351370994909)
XLA Ops:
  0.0 0.7 compare_reduce_fusion
  0.7 0.7 maximum_bitcast_fusion
  1.6 0.6 gather_fusion
  2.2 0.8 broadcast_select_fusion.1
  3.0 7.3 %all-to-all-start = ((bf16[8,2,2048]{2,1,0:T(2,128)(2,1)}), bf16[8,2,2048]{2,1,0:T(2,128)(2,1)S(1)}, u32[]{:S(2)}, u32[]{:S(2)}) async-start(bf16[8,2,2048]{2,1,0:T(2,128)(2,1)} %broadcast_select_fusion.1), calls=%async_computation | async-start | bytes 131072 | tf_op jit(solution)/shard_map/all_to_all | solution.py:84
  10.3 0.8 reduce-window.9
  11.1 0.7 bitcast_subtract_fusion
  11.8 1.3 dynamic_slice.18
  13.0 0.7 dynamic_slice.17
  13.7 0.7 add_add_fusion
  14.4 1.1 fusion.36
  15.5 0.6 iota_compare_fusion
  16.5 0.7 all-to-all-done
  17.2 5.8 %all_gather.3 = bf16[64,2048]{1,0:T(8,128)(2,1)S(1)} all-gather(bf16[16,2048]{1,0:T(8,128)(2,1)S(1)} %all_to_all.20), channel_id=1, replica_groups=mesh['vol'=8,'nar'=4] {'nar'}, dimensions={0}, use_global_device_ids=true | all-gather | bytes 327680 | tf_op jit(solution)/shard_map/all_gather | solution.py:91
  23.5 10.0 %reshape.598 = bf16[64,4,128,2]{1,0,3,2:T(8,128)(2,1)} reshape(bf16[256,256]{0,1:T(8,128)(2,1)S(1)} %copy.27) | data formatting | bytes 262144 | tf_op jit(solution)/shard_map/reshape | solution.py:96
  33.5 6.2 %copy.28 = bf16[128,4,2,64]{0,3,2,1:T(8,128)(2,1)S(1)} copy(bf16[128,4,2,64]{1,3,2,0:T(8,128)(2,1)} %bitcast.64) | data formatting | bytes 262144 | tf_op jit(solution)/shard_map/transpose | solution.py:97
  39.9 0.9 reshape.631
  40.8 5.4 %all-to-all-start.1 = ((bf16[8,2,4096]{2,1,0:T(2,128)(2,1)}), bf16[8,2,4096]{2,1,0:T(2,128)(2,1)S(1)}, u32[]{:S(2)}, u32[]{:S(2)}) async-start(bf16[8,2,4096]{2,1,0:T(2,128)(2,1)} %reshape.631), calls=%async_computation.1 | async-start | bytes 262144 | tf_op jit(solution)/shard_map/all_to_all | solution.py:112
  47.0 6.6 %all-to-all-done.1 = bf16[8,2,4096]{2,1,0:T(2,128)(2,1)S(1)} async-done(((bf16[8,2,4096]{2,1,0:T(2,128)(2,1)}), bf16[8,2,4096]{2,1,0:T(2,128)(2,1)S(1)}, u32[]{:S(2)}, u32[]{:S(2)}) %all-to-all-start.1) | async-done | bytes 131104 | tf_op jit(solution)/shard_map/all_to_all | solution.py:112
  54.3 78.9 %while.19 = (s32[]{:T(128)}, f32[16,2,512]{2,1,0:T(2,128)S(1)}, f32[512]{0:T(512)S(1)}, f32[512]{0:T(512)S(1)}, f32[512]{0:T(512)S(1)}, /*index=5*/bf16[16,8,512...) while((s32[]{:T(128)}, f32[16,2,512]{2,1,0:T(2,128)S(1)}, ...), condition=%wide.region_4.5_spmd.clone.clone.clone, body=%wide.region_1.4_spmd.clone.clone.clone.sunk | while | flops 22971540 | bytes 8845429 | solution.py:125
  54.6 7.8 %fusion.56 = (bf16[16,512,64]{1,2,0:T(8,128)(2,1)S(1)}, bf16[16,512,64]{1,2,0:T(8,128)(2,1)S(1)}) fusion(f32[512,64]{0,1:T(8,128)S(1)} %multiply_add_fusion.2, f32[16]{0:T(128)S(1)} %fusion.55), kind=kLoop, calls=%fused_computation.5.clone.1 | loop fusion | flops 1572864 | bytes 2228288 | tf_op jit(solution)/shard_map/convert
  62.4 0.4 fusion.57
  64.5 7.8 %fusion.56 = (bf16[16,512,64]{1,2,0:T(8,128)(2,1)S(1)}, bf16[16,512,64]{1,2,0:T(8,128)(2,1)S(1)}) fusion(f32[512,64]{0,1:T(8,128)S(1)} %multiply_add_fusion.2, f32[16]{0:T(128)S(1)} %fusion.55), kind=kLoop, calls=%fused_computation.5.clone.1 | loop fusion | flops 1572864 | bytes 2228288 | tf_op jit(solution)/shard_map/convert
  72.2 0.4 fusion.57
  74.3 7.8 %fusion.56 = (bf16[16,512,64]{1,2,0:T(8,128)(2,1)S(1)}, bf16[16,512,64]{1,2,0:T(8,128)(2,1)S(1)}) fusion(f32[512,64]{0,1:T(8,128)S(1)} %multiply_add_fusion.2, f32[16]{0:T(128)S(1)} %fusion.55), kind=kLoop, calls=%fused_computation.5.clone.1 | loop fusion | flops 1572864 | bytes 2228288 | tf_op jit(solution)/shard_map/convert
  82.1 0.4 fusion.57
  84.2 7.8 %fusion.56 = (bf16[16,512,64]{1,2,0:T(8,128)(2,1)S(1)}, bf16[16,512,64]{1,2,0:T(8,128)(2,1)S(1)}) fusion(f32[512,64]{0,1:T(8,128)S(1)} %multiply_add_fusion.2, f32[16]{0:T(128)S(1)} %fusion.55), kind=kLoop, calls=%fused_computation.5.clone.1 | loop fusion | flops 1572864 | bytes 2228288 | tf_op jit(solution)/shard_map/convert
  94.1 7.8 %fusion.56 = (bf16[16,512,64]{1,2,0:T(8,128)(2,1)S(1)}, bf16[16,512,64]{1,2,0:T(8,128)(2,1)S(1)}) fusion(f32[512,64]{0,1:T(8,128)S(1)} %multiply_add_fusion.2, f32[16]{0:T(128)S(1)} %fusion.55), kind=kLoop, calls=%fused_computation.5.clone.1 | loop fusion | flops 1572864 | bytes 2228288 | tf_op jit(solution)/shard_map/convert
  103.9 7.8 %fusion.56 = (bf16[16,512,64]{1,2,0:T(8,128)(2,1)S(1)}, bf16[16,512,64]{1,2,0:T(8,128)(2,1)S(1)}) fusion(f32[512,64]{0,1:T(8,128)S(1)} %multiply_add_fusion.2, f32[16]{0:T(128)S(1)} %fusion.55), kind=kLoop, calls=%fused_computation.5.clone.1 | loop fusion | flops 1572864 | bytes 2228288 | tf_op jit(solution)/shard_map/convert
  113.8 7.8 %fusion.56 = (bf16[16,512,64]{1,2,0:T(8,128)(2,1)S(1)}, bf16[16,512,64]{1,2,0:T(8,128)(2,1)S(1)}) fusion(f32[512,64]{0,1:T(8,128)S(1)} %multiply_add_fusion.2, f32[16]{0:T(128)S(1)} %fusion.55), kind=kLoop, calls=%fused_computation.5.clone.1 | loop fusion | flops 1572864 | bytes 2228288 | tf_op jit(solution)/shard_map/convert
  123.6 7.8 %fusion.56 = (bf16[16,512,64]{1,2,0:T(8,128)(2,1)S(1)}, bf16[16,512,64]{1,2,0:T(8,128)(2,1)S(1)}) fusion(f32[512,64]{0,1:T(8,128)S(1)} %multiply_add_fusion.2, f32[16]{0:T(128)S(1)} %fusion.55), kind=kLoop, calls=%fused_computation.5.clone.1 | loop fusion | flops 1572864 | bytes 2228288 | tf_op jit(solution)/shard_map/convert
  133.2 0.6 copy-done.1
  (155 shorter events, 16.6 us)
Async XLA Ops:
  0.0 1.6 %copy-start = (bf16[64,2048]{1,0:T(8,128)(2,1)S(1)}, bf16[64,2048]{1,0:T(8,128)(2,1)}, u32[]{:S(2)}) copy-start(bf16[64,2048]{1,0:T(8,128)(2,1)} %param.6) | copy-start | bytes 786436
  3.0 14.2 %all-to-all-start = ((bf16[8,2,2048]{2,1,0:T(2,128)(2,1)}), bf16[8,2,2048]{2,1,0:T(2,128)(2,1)S(1)}, u32[]{:S(2)}, u32[]{:S(2)}) async-start(bf16[8,2,2048]{2,1,0:T(2,128)(2,1)} %broadcast_select_fusion.1), calls=%async_computation | async-start | bytes 131072 | tf_op jit(solution)/shard_map/all_to_all | solution.py:84
  33.5 13.4 %copy-start.2 = (s32[2,512]{1,0:T(2,128)S(1)}, s32[2,512]{1,0:T(2,128)}, u32[]{:S(2)}) copy-start(s32[2,512]{1,0:T(2,128)} %param.9) | copy-start | bytes 12292
  40.8 12.9 %all-to-all-start.1 = ((bf16[8,2,4096]{2,1,0:T(2,128)(2,1)}), bf16[8,2,4096]{2,1,0:T(2,128)(2,1)S(1)}, u32[]{:S(2)}, u32[]{:S(2)}) async-start(bf16[8,2,4096]{2,1,0:T(2,128)(2,1)} %reshape.631), calls=%async_computation.1 | async-start | bytes 262144 | tf_op jit(solution)/shard_map/all_to_all | solution.py:112
  133.2 0.6 copy-start.1
where the time goes:
time: 134 us
  other arithmetic  78 us (58%)
  local copies, waits for them, and re-layouts  24.5 us (18%)
  starting transfers between devices  12.6 us (9%)
  waiting for transfers between devices  7.29 us (5%)
  blocking collectives  5.78 us (4%)
  matrix products  3.81 us (3%)
    another operation x9, other arithmetic  63 us
    reshape x1, local copies, waits for them, and re-layouts, per_device(): (spectral * dft_scale).astype(jnp.bfloat16)  9.98 us
    all_to_all x1, starting transfers between devices, per_device(): lax.all_to_all(packed, 'vol', split_axis=0, concat_axis=0, tiled=True)  7.28 us
    all_to_all x1, waiting for transfers between devices, per_device(): lax.all_to_all(spectra, 'vol', split_axis=0, concat_axis=2, tiled=True)  6.64 us
    transpose x1, local copies, waits for them, and re-layouts, per_device(): spectra = spectral.transpose(2, 1, 3, 0).reshape(bin_cap, 2 * NQ, rows_here)  6.2 us
    all_gather x1, blocking collectives, per_device(): row_piece = lax.all_gather(arrived, 'nar', axis=0, tiled=True)  5.78 us
    all_to_all x1, starting transfers between devices, per_device(): lax.all_to_all(spectra, 'vol', split_axis=0, concat_axis=2, tiled=True)  5.37 us
    dot_general x8, matrix products, apply_green(): jnp.einsum('bxp,bcp->bxc', green_grid, spec_block, preferred_element_type...  3.55 us
  transfers between devices with their start and end apart: 2, of which 2 were waited for; matrix products, arithmetic and copies ran while one was open for 5% of the time, Pallas kernels for 0%

commit v1 on v0

--- a/solution.py
+++ b/solution.py
@@ -7,6 +7,22 @@
 NF = 256
 NQ = 4
 WAVE_STEP = 0.05
+
+
+def exchange_in_pairs(shard, axis, split, join):
+    ways, here = (lax.axis_size(axis), lax.axis_index(axis))
+    width = shard.shape[split] // ways
+    lengths = list(shard.shape)
+    lengths[split] = width
+    height = lengths[join]
+    lengths[join] = height * ways
+    full = jnp.zeros(lengths, shard.dtype)
+    for mask in range(ways):
+        part = lax.dynamic_slice_in_dim(shard, (here ^ mask) * width, width, axis=split)
+        if mask:
+            part = lax.ppermute(part, axis, [(d, d ^ mask) for d in range(ways)])
+        full = lax.dynamic_update_slice_in_dim(full, part, (here ^ mask) * height, axis=join)
+    return full
 
 
 def dft_table(bin_ids, keep_bin, time_len):
@@ -109,7 +125,7 @@
     norm_scale = 1.0 / math.sqrt(vol_count * nar_count * slot_total)
     facing = directions(observer_cells)
     share_rows = bin_cap // vol_count
-    regrouped = lax.all_to_all(spectra, "vol", split_axis=0, concat_axis=2, tiled=True)
+    regrouped = exchange_in_pairs(spectra, "vol", 0, 2)
     bin_ids = own_start + vol_index * share_rows + jnp.arange(share_rows, dtype=jnp.int32)
     span_points = local_points * max(1, vol_count // 8)
     turn_count = vol_count * local_points // span_points

time: 134 us -> 151 us (1.13)
  local copies, waits for them, and re-layouts: 24.5 us -> 35.4 us
  starting transfers between devices: 12.6 us -> 18.2 us
    dynamic_update_slice x0 -> x8, local copies, waits for them, and re-layouts: none -> 11.3 us  [exchange_in_pairs(): lax.dynamic_update_slice_in_dim(full, part, (here ^ mask) * height, axis=...]
    ppermute x0 -> x7, starting transfers between devices: none -> 11 us  [exchange_in_pairs(): part = lax.ppermute(part, axis, [(d, d ^ mask) for d in range(ways)])]
    all_to_all x1 -> x0, waiting for transfers between devices: 6.64 us -> none  [per_device(): lax.all_to_all(spectra, 'vol', split_axis=0, concat_axis=2, tiled=True)]
    ppermute x0 -> x7, waiting for transfers between devices: none -> 6.45 us  [exchange_in_pairs(): part = lax.ppermute(part, axis, [(d, d ^ mask) for d in range(ways)])]
    all_to_all x1 -> x0, starting transfers between devices: 5.37 us -> none  [per_device(): lax.all_to_all(spectra, 'vol', split_axis=0, concat_axis=2, tiled=True)]
  transfers between devices with their start and end apart: 2 -> 8, of which waited for: 2 -> 3; matrix products, arithmetic and copies ran while one was open for 5% -> 10% of each run, Pallas kernels for 0% -> 0%
where the time goes in v1:
time: 151 us; the launch traced here: 150 us
  other arithmetic  77.9 us (52%)
  local copies, waits for them, and re-layouts  35.4 us (23%)
  starting transfers between devices  18.2 us (12%)
  waiting for transfers between devices  7.26 us (5%)
  blocking collectives  5.78 us (4%)
  matrix products  3.81 us (3%)
    another operation x9, other arithmetic  63 us
    dynamic_update_slice x8, local copies, waits for them, and re-layouts, exchange_in_pairs(): lax.dynamic_update_slice_in_dim(full, part, (here ^ mask) * height, axis=...  11.3 us
    ppermute x7, starting transfers between devices, exchange_in_pairs(): part = lax.ppermute(part, axis, [(d, d ^ mask) for d in range(ways)])  11 us
    reshape x1, local copies, waits for them, and re-layouts, per_device(): (spectral * dft_scale).astype(jnp.bfloat16)  9.98 us
    all_to_all x1, starting transfers between devices, per_device(): lax.all_to_all(packed, 'vol', split_axis=0, concat_axis=0, tiled=True)  7.28 us
    ppermute x7, waiting for transfers between devices, exchange_in_pairs(): part = lax.ppermute(part, axis, [(d, d ^ mask) for d in range(ways)])  6.45 us
    transpose x1, local copies, waits for them, and re-layouts, per_device(): spectra = spectral.transpose(2, 1, 3, 0).reshape(bin_cap, 2 * NQ, rows_here)  6.19 us
    all_gather x1, blocking collectives, per_device(): row_piece = lax.all_gather(arrived, 'nar', axis=0, tiled=True)  5.78 us
  transfers between devices with their start and end apart: 8, of which 3 were waited for; matrix products, arithmetic and copies ran while one was open for 10% of the time, Pallas kernels for 0%

profile of v1, /device:TPU:0, one launch (start us, length us, event | category | flops | bytes accessed | tf_op | source)
XLA Modules:
  0.0 150.3 jit_solution(2405852489423786159)
XLA Ops:
  0.0 0.7 compare_reduce_fusion
  2.2 0.8 broadcast_select_fusion.1
  3.0 7.3 %all-to-all-start = ((bf16[8,2,2048]{2,1,0:T(2,128)(2,1)}), bf16[8,2,2048]{2,1,0:T(2,128)(2,1)S(1)}, u32[]{:S(2)}, u32[]{:S(2)}) async-start(bf16[8,2,2048]{2,1,0:T(2,128)(2,1)} %broadcast_select_fusion.1), calls=%async_computation | async-start | bytes 131072 | tf_op jit(solution)/shard_map/all_to_all | solution.py:100
  10.3 0.8 reduce-window.9
  11.1 0.7 bitcast_subtract_fusion
  11.8 1.2 dynamic_slice.42
  14.2 1.1 fusion.36
  16.4 0.8 all-to-all-done
  17.2 5.8 %all_gather.3 = bf16[64,2048]{1,0:T(8,128)(2,1)S(1)} all-gather(bf16[16,2048]{1,0:T(8,128)(2,1)S(1)} %all_to_all.7), channel_id=1, replica_groups=mesh['vol'=8,'nar'=4] {'nar'}, dimensions={0}, use_global_device_ids=true | all-gather | bytes 327680 | tf_op jit(solution)/shard_map/all_gather | solution.py:107
  23.5 10.0 %reshape.598 = bf16[64,4,128,2]{1,0,3,2:T(8,128)(2,1)} reshape(bf16[256,256]{0,1:T(8,128)(2,1)S(1)} %copy.26) | data formatting | bytes 262144 | tf_op jit(solution)/shard_map/reshape | solution.py:112
  33.5 6.2 %copy.27 = bf16[128,4,2,64]{0,3,2,1:T(8,128)(2,1)S(1)} copy(bf16[128,4,2,64]{1,3,2,0:T(8,128)(2,1)} %bitcast.59) | data formatting | bytes 262144 | tf_op jit(solution)/shard_map/transpose | solution.py:113
  40.2 1.3 collective-permute-start
  41.5 1.5 collective-permute-start.1
  42.9 0.8 collective-permute-start.2
  43.7 2.1 %collective-permute-start.3 = (bf16[16,8,64]{0,2,1:T(8,128)(2,1)S(1)}, bf16[16,8,64]{0,2,1:T(8,128)(2,1)S(1)}, u32[]{:S(2)}, u32[]{:S(2)}) collective-permute-start(bf16[16,8,64]{0,2,1:T(8,128)(2,1)S(1)} %get-tuple-element.352), channel_id=1, source_target_pairs={{0,16},{4,20},{8,24},{12,28},{16,0},{20,4},{24,8},{28,12},{1,17},{... | collective-permute-start | bytes 49160 | tf_op jit(solution)/shard_map/ppermute | solution.py:23
  45.8 1.5 collective-permute-start.4
  47.3 3.3 %collective-permute-start.5 = (bf16[16,8,64]{0,2,1:T(8,128)(2,1)S(1)}, bf16[16,8,64]{0,2,1:T(8,128)(2,1)S(1)}, u32[]{:S(2)}, u32[]{:S(2)}) collective-permute-start(bf16[16,8,64]{0,2,1:T(8,128)(2,1)S(1)} %get-tuple-element.350), channel_id=1, source_target_pairs={{0,24},{4,28},{8,16},{12,20},{16,8},{20,12},{24,0},{28,4},{1,25},{... | collective-permute-start | bytes 49160 | tf_op jit(solution)/shard_map/ppermute | solution.py:23
  50.6 1.7 %collective-permute-done.1 = bf16[16,8,64]{0,2,1:T(8,128)(2,1)S(1)} collective-permute-done((bf16[16,8,64]{0,2,1:T(8,128)(2,1)S(1)}, bf16[16,8,64]{0,2,1:T(8,128)(2,1)S(1)}, u32[]{:S(2)}, u32[]{:S(2)}) %collective-permute-start.1) | collective-permute-done | bytes 16416 | tf_op jit(solution)/shard_map/ppermute | solution.py:23
  54.3 2.5 %dynamic_update_slice.25 = bf16[16,8,512]{2,1,0:T(8,128)(2,1)S(1)} dynamic-update-slice(bf16[16,8,512]{2,1,0:T(8,128)(2,1)S(1)} %dynamic_update_slice.24, bf16[16,8,64]{2,1,0:T(8,128)(2,1)S(1)} %copy.29, s32[]{:T(128)} %constant.416.clone.1, s32[]{:T(128)} %constant.416.clone.1, s32[]{:T(128)S(6)} %select_n.392) | dynamic-update-slice | bytes 32772 | tf_op jit(solution)/shard_map/dynamic_update_slice | solution.py:24
  57.4 2.5 %dynamic_update_slice.27 = bf16[16,8,512]{2,1,0:T(8,128)(2,1)S(1)} dynamic-update-slice(bf16[16,8,512]{2,1,0:T(8,128)(2,1)S(1)} %dynamic_update_slice.26, bf16[16,8,64]{2,1,0:T(8,128)(2,1)S(1)} %copy.31, s32[]{:T(128)} %constant.416.clone.1, s32[]{:T(128)} %constant.416.clone.1, s32[]{:T(128)S(6)} %select_n.396) | dynamic-update-slice | bytes 32772 | tf_op jit(solution)/shard_map/dynamic_update_slice | solution.py:24
  60.4 4.7 %collective-permute-done.4 = bf16[16,8,64]{0,2,1:T(8,128)(2,1)S(1)} collective-permute-done((bf16[16,8,64]{0,2,1:T(8,128)(2,1)S(1)}, bf16[16,8,64]{0,2,1:T(8,128)(2,1)S(1)}, u32[]{:S(2)}, u32[]{:S(2)}) %collective-permute-start.4) | collective-permute-done | bytes 16416 | tf_op jit(solution)/shard_map/ppermute | solution.py:23
  65.2 2.5 %dynamic_update_slice.29 = bf16[16,8,512]{2,1,0:T(8,128)(2,1)S(1)} dynamic-update-slice(bf16[16,8,512]{2,1,0:T(8,128)(2,1)S(1)} %dynamic_update_slice.28, bf16[16,8,64]{2,1,0:T(8,128)(2,1)S(1)} %copy.33, s32[]{:T(128)} %constant.416.clone.1, s32[]{:T(128)} %constant.416.clone.1, s32[]{:T(128)S(6)} %select_n.400) | dynamic-update-slice | bytes 32772 | tf_op jit(solution)/shard_map/dynamic_update_slice | solution.py:24
  68.3 2.5 %dynamic_update_slice.31 = bf16[16,8,512]{2,1,0:T(8,128)(2,1)S(1)} dynamic-update-slice(bf16[16,8,512]{2,1,0:T(8,128)(2,1)S(1)} %dynamic_update_slice.30, bf16[16,8,64]{2,1,0:T(8,128)(2,1)S(1)} %copy.35, s32[]{:T(128)} %constant.416.clone.1, s32[]{:T(128)} %constant.416.clone.1, s32[]{:T(128)S(6)} %select_n.404) | dynamic-update-slice | bytes 32772 | tf_op jit(solution)/shard_map/dynamic_update_slice | solution.py:24
  70.8 78.9 %while.19 = (s32[]{:T(128)}, f32[16,2,512]{2,1,0:T(2,128)S(1)}, f32[512]{0:T(512)S(1)}, f32[512]{0:T(512)S(1)}, f32[512]{0:T(512)S(1)}, /*index=5*/bf16[16,8,512...) while((s32[]{:T(128)}, f32[16,2,512]{2,1,0:T(2,128)S(1)}, ...), condition=%wide.region_4.5_spmd.clone.clone.clone, body=%wide.region_1.4_spmd.clone.clone.clone.sunk | while | flops 22971540 | bytes 8845429 | solution.py:141
  71.1 7.8 %fusion.56 = (bf16[16,512,64]{1,2,0:T(8,128)(2,1)S(1)}, bf16[16,512,64]{1,2,0:T(8,128)(2,1)S(1)}) fusion(f32[512,64]{0,1:T(8,128)S(1)} %multiply_add_fusion.2, f32[16]{0:T(128)S(1)} %fusion.55), kind=kLoop, calls=%fused_computation.5.clone.1 | loop fusion | flops 1572864 | bytes 2228288 | tf_op jit(solution)/shard_map/convert
  80.9 7.8 %fusion.56 = (bf16[16,512,64]{1,2,0:T(8,128)(2,1)S(1)}, bf16[16,512,64]{1,2,0:T(8,128)(2,1)S(1)}) fusion(f32[512,64]{0,1:T(8,128)S(1)} %multiply_add_fusion.2, f32[16]{0:T(128)S(1)} %fusion.55), kind=kLoop, calls=%fused_computation.5.clone.1 | loop fusion | flops 1572864 | bytes 2228288 | tf_op jit(solution)/shard_map/convert
  90.8 7.8 %fusion.56 = (bf16[16,512,64]{1,2,0:T(8,128)(2,1)S(1)}, bf16[16,512,64]{1,2,0:T(8,128)(2,1)S(1)}) fusion(f32[512,64]{0,1:T(8,128)S(1)} %multiply_add_fusion.2, f32[16]{0:T(128)S(1)} %fusion.55), kind=kLoop, calls=%fused_computation.5.clone.1 | loop fusion | flops 1572864 | bytes 2228288 | tf_op jit(solution)/shard_map/convert
  100.7 7.8 %fusion.56 = (bf16[16,512,64]{1,2,0:T(8,128)(2,1)S(1)}, bf16[16,512,64]{1,2,0:T(8,128)(2,1)S(1)}) fusion(f32[512,64]{0,1:T(8,128)S(1)} %multiply_add_fusion.2, f32[16]{0:T(128)S(1)} %fusion.55), kind=kLoop, calls=%fused_computation.5.clone.1 | loop fusion | flops 1572864 | bytes 2228288 | tf_op jit(solution)/shard_map/convert
  110.5 7.8 %fusion.56 = (bf16[16,512,64]{1,2,0:T(8,128)(2,1)S(1)}, bf16[16,512,64]{1,2,0:T(8,128)(2,1)S(1)}) fusion(f32[512,64]{0,1:T(8,128)S(1)} %multiply_add_fusion.2, f32[16]{0:T(128)S(1)} %fusion.55), kind=kLoop, calls=%fused_computation.5.clone.1 | loop fusion | flops 1572864 | bytes 2228288 | tf_op jit(solution)/shard_map/convert
  120.4 7.8 %fusion.56 = (bf16[16,512,64]{1,2,0:T(8,128)(2,1)S(1)}, bf16[16,512,64]{1,2,0:T(8,128)(2,1)S(1)}) fusion(f32[512,64]{0,1:T(8,128)S(1)} %multiply_add_fusion.2, f32[16]{0:T(128)S(1)} %fusion.55), kind=kLoop, calls=%fused_computation.5.clone.1 | loop fusion | flops 1572864 | bytes 2228288 | tf_op jit(solution)/shard_map/convert
  130.3 7.8 %fusion.56 = (bf16[16,512,64]{1,2,0:T(8,128)(2,1)S(1)}, bf16[16,512,64]{1,2,0:T(8,128)(2,1)S(1)}) fusion(f32[512,64]{0,1:T(8,128)S(1)} %multiply_add_fusion.2, f32[16]{0:T(128)S(1)} %fusion.55), kind=kLoop, calls=%fused_computation.5.clone.1 | loop fusion | flops 1572864 | bytes 2228288 | tf_op jit(solution)/shard_map/convert
  140.1 7.8 %fusion.56 = (bf16[16,512,64]{1,2,0:T(8,128)(2,1)S(1)}, bf16[16,512,64]{1,2,0:T(8,128)(2,1)S(1)}) fusion(f32[512,64]{0,1:T(8,128)S(1)} %multiply_add_fusion.2, f32[16]{0:T(128)S(1)} %fusion.55), kind=kLoop, calls=%fused_computation.5.clone.1 | loop fusion | flops 1572864 | bytes 2228288 | tf_op jit(solution)/shard_map/convert
  (180 shorter events, 24.0 us)
Async XLA Ops:
  0.0 1.6 %copy-start = (bf16[64,2048]{1,0:T(8,128)(2,1)S(1)}, bf16[64,2048]{1,0:T(8,128)(2,1)}, u32[]{:S(2)}) copy-start(bf16[64,2048]{1,0:T(8,128)(2,1)} %param.6) | copy-start | bytes 786436
  3.0 14.2 %all-to-all-start = ((bf16[8,2,2048]{2,1,0:T(2,128)(2,1)}), bf16[8,2,2048]{2,1,0:T(2,128)(2,1)S(1)}, u32[]{:S(2)}, u32[]{:S(2)}) async-start(bf16[8,2,2048]{2,1,0:T(2,128)(2,1)} %broadcast_select_fusion.1), calls=%async_computation | async-start | bytes 131072 | tf_op jit(solution)/shard_map/all_to_all | solution.py:100
  39.7 13.2 %copy-start.2 = (s32[2,512]{1,0:T(2,128)S(1)}, s32[2,512]{1,0:T(2,128)}, u32[]{:S(2)}) copy-start(s32[2,512]{1,0:T(2,128)} %param.9) | copy-start | bytes 12292
  40.2 7.1 %collective-permute-start = (bf16[16,8,64]{0,2,1:T(8,128)(2,1)S(1)}, bf16[16,8,64]{0,2,1:T(8,128)(2,1)S(1)}, u32[]{:S(2)}, u32[]{:S(2)}) collective-permute-start(bf16[16,8,64]{0,2,1:T(8,128)(2,1)S(1)} %get-tuple-element.355), channel_id=1, source_target_pairs={{0,4},{4,0},{8,12},{12,8},{16,20},{20,16},{24,28},{28,24},{1,5},{5... | collective-permute-start | bytes 49160 | tf_op jit(solution)/shard_map/ppermute | solution.py:23
  41.5 10.9 %collective-permute-start.1 = (bf16[16,8,64]{0,2,1:T(8,128)(2,1)S(1)}, bf16[16,8,64]{0,2,1:T(8,128)(2,1)S(1)}, u32[]{:S(2)}, u32[]{:S(2)}) collective-permute-start(bf16[16,8,64]{0,2,1:T(8,128)(2,1)S(1)} %get-tuple-element.354), channel_id=1, source_target_pairs={{0,8},{4,12},{8,0},{12,4},{16,24},{20,28},{24,16},{28,20},{1,9},{5... | collective-permute-start | bytes 49160 | tf_op jit(solution)/shard_map/ppermute | solution.py:23
  42.9 14.4 %collective-permute-start.2 = (bf16[16,8,64]{0,2,1:T(8,128)(2,1)S(1)}, bf16[16,8,64]{0,2,1:T(8,128)(2,1)S(1)}, u32[]{:S(2)}, u32[]{:S(2)}) collective-permute-start(bf16[16,8,64]{0,2,1:T(8,128)(2,1)S(1)} %get-tuple-element.353), channel_id=1, source_target_pairs={{0,12},{4,8},{8,4},{12,0},{16,28},{20,24},{24,20},{28,16},{1,13},{... | collective-permute-start | bytes 49160 | tf_op jit(solution)/shard_map/ppermute | solution.py:23
  43.7 16.2 %collective-permute-start.3 = (bf16[16,8,64]{0,2,1:T(8,128)(2,1)S(1)}, bf16[16,8,64]{0,2,1:T(8,128)(2,1)S(1)}, u32[]{:S(2)}, u32[]{:S(2)}) collective-permute-start(bf16[16,8,64]{0,2,1:T(8,128)(2,1)S(1)} %get-tuple-element.352), channel_id=1, source_target_pairs={{0,16},{4,20},{8,24},{12,28},{16,0},{20,4},{24,8},{28,12},{1,17},{... | collective-permute-start | bytes 49160 | tf_op jit(solution)/shard_map/ppermute | solution.py:23
  45.8 19.2 %collective-permute-start.4 = (bf16[16,8,64]{0,2,1:T(8,128)(2,1)S(1)}, bf16[16,8,64]{0,2,1:T(8,128)(2,1)S(1)}, u32[]{:S(2)}, u32[]{:S(2)}) collective-permute-start(bf16[16,8,64]{0,2,1:T(8,128)(2,1)S(1)} %get-tuple-element.351), channel_id=1, source_target_pairs={{0,20},{4,16},{8,28},{12,24},{16,4},{20,0},{24,12},{28,8},{1,21},{... | collective-permute-start | bytes 49160 | tf_op jit(solution)/shard_map/ppermute | solution.py:23
  47.3 20.4 %collective-permute-start.5 = (bf16[16,8,64]{0,2,1:T(8,128)(2,1)S(1)}, bf16[16,8,64]{0,2,1:T(8,128)(2,1)S(1)}, u32[]{:S(2)}, u32[]{:S(2)}) collective-permute-start(bf16[16,8,64]{0,2,1:T(8,128)(2,1)S(1)} %get-tuple-element.350), channel_id=1, source_target_pairs={{0,24},{4,28},{8,16},{12,20},{16,8},{20,12},{24,0},{28,4},{1,25},{... | collective-permute-start | bytes 49160 | tf_op jit(solution)/shard_map/ppermute | solution.py:23
  52.3 15.8 %collective-permute-start.6 = (bf16[16,8,64]{0,2,1:T(8,128)(2,1)S(1)}, bf16[16,8,64]{0,2,1:T(8,128)(2,1)S(1)}, u32[]{:S(2)}, u32[]{:S(2)}) collective-permute-start(bf16[16,8,64]{0,2,1:T(8,128)(2,1)S(1)} %get-tuple-element.349), channel_id=1, source_target_pairs={{0,28},{4,24},{8,20},{12,16},{16,12},{20,8},{24,4},{28,0},{1,29},{... | collective-permute-start | bytes 49160 | tf_op jit(solution)/shard_map/ppermute | solution.py:23
  149.7 0.6 copy-start.1
